TPU v7x, 32 devices: a whole 2x2x4 slice. The times are simulated.
32 devices in a mesh: fsdp: 2 (over x), ctx: 4 (over y, core), tp: 4 (over z).
Axes of the slice: x: 2, y: 2, z: 4, core: 2. Of those that a mesh axis runs over, the one named last changes fastest.
Arguments:
- tokens: bfloat16 [8, 512, 768], P(('fsdp', 'tp'), 'ctx'), may hold values from -6 to 6
- seg_ids: int32 [8, 512], P(('fsdp', 'tp')), may hold values from 0 to 2, never falling along the last dimension, each value on 1 to 384 neighbouring positions
- routes: int32 [8, 512, 2], P(('fsdp', 'tp'), 'ctx'), may hold values from 0 to 3, all different within a row; in each aligned block of 128 rows (0 to 127, 128 to 255, ..., all dimensions but the last counted through in order) at most 80 rows name the same one
- norm_attn: bfloat16 [768], P('fsdp'), may hold values from 0.5 to 1.5
- weight_qkv: bfloat16 [768, 2304], P('fsdp'), may hold values from -0.21875 to 0.21875
- weight_proj: bfloat16 [768, 768], P(None, 'fsdp'), may hold values from -0.875 to 0.875
- rel_table: float32 [12, 32], replicated, may hold values from -4 to 4
- norm_ffn: bfloat16 [768], P('fsdp'), may hold values from 0.5 to 1.5
- weight_router: bfloat16 [768, 4], P('fsdp'), may hold values from -0.21875 to 0.21875
- expert_up: bfloat16 [4, 768, 3072], P(None, 'fsdp', ('ctx', 'tp')), may hold values from -0.21875 to 0.21875
- expert_down: bfloat16 [4, 3072, 768], P(None, ('ctx', 'tp'), 'fsdp'), may hold values from -0.109375 to 0.109375
- cotangent: bfloat16 [8, 512, 768], P(('fsdp', 'tp'), 'ctx'), may hold values from -6 to 6
Outputs:
- output: bfloat16 [8, 512, 768], P(('fsdp', 'tp'), 'ctx')
- grad_tokens: float32 [8, 512, 768], P(('fsdp', 'tp'), 'ctx')
- grad_norm_attn: float32 [768], P('fsdp')
- grad_weight_qkv: float32 [768, 2304], P('fsdp')
- grad_weight_proj: float32 [768, 768], P(None, 'fsdp')
- grad_rel_table: float32 [12, 32], replicated
- grad_norm_ffn: float32 [768], P('fsdp')
- grad_weight_router: float32 [768, 4], P('fsdp')
- grad_expert_up: float32 [4, 768, 3072], P(None, 'fsdp', ('ctx', 'tp'))
- grad_expert_down: float32 [4, 3072, 768], P(None, ('ctx', 'tp'), 'fsdp')
Inputs may be any that keep to these rules, and one draw needn't show every extreme that they name: `seg_ids`: each group's 512 positions fall into at most 3 sequences whose numbers never fall along the positions; the longest has exactly 384 positions. `routes`: each token names two different experts. In each aligned block of 128 rows (the rows of one device) no expert is named more than 80 times, and in every draw some expert is named exactly 80 times in some block.
All inputs are finite; a program needn't handle non-finite values.
Results may differ from a plain program's by a relative error of at most 0.012.
Values may be sent and summed in bfloat16 or wider, within the bound.
A program may use at most 192 MiB of HBM per device.

v0:
```python
import jax
import jax.numpy as jnp
import numpy as np
from jax import lax
from jax.sharding import PartitionSpec as P

BUCKETS = 32
MAX_DISTANCE = 128
MOST = 80
EPSILON = 1e-06
MASK_FILL = -1e30


def bucket_bounds(buckets, far_reach):
    exact_count = buckets // 2
    bounds = []
    for number in range(1, buckets):
        if number <= exact_count:
            bounds.append(number)
        else:
            exponent = (number - exact_count) / (buckets - exact_count)
            bounds.append(int(np.ceil(exact_count * (far_reach / exact_count) ** exponent)))
    return np.array(bounds, dtype=np.int32)


def bucket_onehot(length):
    bounds = jnp.asarray(bucket_bounds(BUCKETS, MAX_DISTANCE))
    distance = jnp.arange(length, dtype=jnp.int32)
    which_bucket = jnp.sum((distance[:, None] >= bounds[None, :]).astype(jnp.int32), axis=1)
    return (which_bucket[:, None] == jnp.arange(BUCKETS, dtype=jnp.int32)[None, :]).astype(
        jnp.float32
    )


def spread_diagonals(vectors):
    heads_here, length = vectors.shape
    padded = jnp.concatenate([vectors[:, ::-1], jnp.zeros_like(vectors)], axis=1)
    repeated = jnp.tile(padded, (1, length))
    window = repeated[:, length - 1 : length - 1 + length * (2 * length - 1)]
    return window.reshape(heads_here, length, 2 * length - 1)[:, :, :length]


def slot_tables(route_ids, experts, capacity):
    flat_ids = route_ids.reshape(-1)
    assignments = flat_ids.shape[0]
    member = (flat_ids[:, None] == jnp.arange(experts, dtype=jnp.int32)[None, :]).astype(jnp.int32)
    before = jnp.cumsum(member, axis=0) - member
    slot_index = jnp.sum(before * member, axis=1)
    position = slot_index * experts + flat_ids
    filler = (
        jnp.full((capacity * experts,), assignments, jnp.int32)
        .at[position]
        .set(jnp.arange(assignments, dtype=jnp.int32))
    )
    return (position, filler)


def rms_scale(values):
    return lax.rsqrt(jnp.mean(values * values, axis=-1, keepdims=True) + EPSILON)


def local(
    tokens,
    seg_ids,
    routes,
    norm_attn,
    weight_qkv,
    weight_proj,
    rel_table,
    norm_ffn,
    weight_router,
    expert_up,
    expert_down,
    cotangent,
):
    row_count = tokens.shape[1]
    model_width = tokens.shape[2]
    head_count = rel_table.shape[0]
    head_size = model_width // head_count
    heads_here = head_count // lax.axis_size("ctx")
    expert_count = expert_up.shape[0]
    length = seg_ids.shape[1]
    score_scale = head_size ** (-0.5)
    ctx_index = lax.axis_index("ctx")
    head_width = heads_here * head_size
    gathered = (
        lax.all_gather(norm_attn, "fsdp", axis=0, tiled=True),
        lax.all_gather(weight_qkv, "fsdp", axis=0, tiled=True),
        lax.all_gather(weight_proj, "fsdp", axis=1, tiled=True),
        lax.all_gather(weight_router, "fsdp", axis=0, tiled=True),
        lax.all_gather(norm_ffn, "fsdp", axis=0, tiled=True),
        lax.all_gather(expert_up, "fsdp", axis=1, tiled=True),
        lax.all_gather(expert_down, "fsdp", axis=2, tiled=True),
    )
    gain_one, qkv_full, proj_full, router_full, gain_two, up_full, down_full = gathered
    inputs = tokens[0].astype(jnp.float32)
    scale_one = rms_scale(inputs)
    normed_one = (inputs * scale_one * gain_one.astype(jnp.float32)).astype(jnp.bfloat16)
    projected = jnp.dot(normed_one, qkv_full, preferred_element_type=jnp.float32).astype(
        jnp.bfloat16
    )
    by_head = lax.all_to_all(
        projected.reshape(row_count, 3, head_count, head_size),
        "ctx",
        split_axis=2,
        concat_axis=0,
        tiled=True,
    )
    query_rows = by_head[:, 0]
    key_rows = by_head[:, 1]
    value_rows = by_head[:, 2]
    table_here = lax.dynamic_slice_in_dim(rel_table, ctx_index * heads_here, heads_here, 0)
    onehot = bucket_onehot(length)
    bias_vector = jnp.dot(table_here, onehot.T, precision=lax.Precision.HIGHEST)
    bias_matrix = spread_diagonals(bias_vector)
    positions = jnp.arange(length, dtype=jnp.int32)
    segment = seg_ids[0]
    allowed = (segment[:, None] == segment[None, :]) & (positions[:, None] >= positions[None, :])
    block_count = length // length
    query_blocks = query_rows.reshape(block_count, length, heads_here, head_size)
    bias_blocks = jnp.moveaxis(bias_matrix.reshape(heads_here, block_count, length, length), 1, 0)
    mask_blocks = allowed.reshape(block_count, length, length)

    def block_scores(query_block, bias_block, mask_block):
        products = jnp.einsum(
            "qhd,khd->hqk", query_block, key_rows, preferred_element_type=jnp.float32
        )
        return jnp.where(mask_block[None], products * score_scale + bias_block, MASK_FILL)

    def forward_block(pieces):
        query_block, bias_block, mask_block = pieces
        scores = block_scores(query_block, bias_block, mask_block)
        row_peak = jnp.max(scores, axis=-1, keepdims=True)
        weights = jnp.exp(scores - row_peak)
        row_total = jnp.sum(weights, axis=-1, keepdims=True)
        low_probs = (weights / row_total).astype(jnp.bfloat16)
        attended = jnp.einsum(
            "hqk,khd->qhd", low_probs, value_rows, preferred_element_type=jnp.float32
        ).astype(jnp.bfloat16)
        return (attended, (row_peak + jnp.log(row_total))[..., 0])

    attended_blocks, log_totals = lax.map(forward_block, (query_blocks, bias_blocks, mask_blocks))
    attended_heads = attended_blocks.reshape(length, heads_here, head_size)
    back_tokens = lax.all_to_all(attended_heads, "ctx", split_axis=0, concat_axis=1, tiled=True)
    mixed_heads = back_tokens.reshape(row_count, model_width)
    attention = jnp.dot(mixed_heads, proj_full, preferred_element_type=jnp.float32)
    middle = inputs + attention
    scale_two = rms_scale(middle)
    normed_two = (middle * scale_two * gain_two.astype(jnp.float32)).astype(jnp.bfloat16)
    logits = jnp.dot(normed_two, router_full, preferred_element_type=jnp.float32)
    route_ids = routes[0]
    choose = (
        route_ids[:, :, None] == jnp.arange(expert_count, dtype=jnp.int32)[None, None, :]
    ).astype(jnp.float32)
    picked = jnp.sum(choose * logits[:, None, :], axis=2)
    gate_raw = jnp.exp(picked - jnp.max(picked, axis=1, keepdims=True))
    gate_weights = gate_raw / jnp.sum(gate_raw, axis=1, keepdims=True)
    position, filler = slot_tables(route_ids, expert_count, MOST)
    padded_rows = jnp.concatenate([normed_two, jnp.zeros((1, model_width), jnp.bfloat16)], axis=0)
    dispatched = padded_rows[filler // 2].reshape(MOST, expert_count, model_width)
    arrived = lax.all_gather(dispatched, ("ctx", "tp"), axis=0, tiled=True)
    pre_act = jnp.einsum("sed,edf->sef", arrived, up_full, preferred_element_type=jnp.float32)
    activated = jax.nn.gelu(pre_act).astype(jnp.bfloat16)
    row_block = activated
    expert_result = lax.psum_scatter(
        jnp.einsum("sef,efd->sed", row_block, down_full, preferred_element_type=jnp.float32),
        ("ctx", "tp"),
        scatter_dimension=0,
        tiled=True,
    )
    per_choice = expert_result.reshape(MOST * expert_count, model_width)[position].reshape(
        row_count, 2, model_width
    )
    result = middle + jnp.sum(gate_weights[:, :, None] * per_choice, axis=1)
    output = result.astype(jnp.bfloat16)[None]
    again = (
        lax.all_gather(norm_attn, "fsdp", axis=0, tiled=True),
        lax.all_gather(weight_qkv, "fsdp", axis=0, tiled=True),
        lax.all_gather(weight_proj, "fsdp", axis=1, tiled=True),
        lax.all_gather(weight_router, "fsdp", axis=0, tiled=True),
        lax.all_gather(norm_ffn, "fsdp", axis=0, tiled=True),
        lax.all_gather(expert_up, "fsdp", axis=1, tiled=True),
        lax.all_gather(expert_down, "fsdp", axis=2, tiled=True),
    )
    gain_first, qkv_again, proj_again, router_again, gain_second, up_again, down_again = again
    grad_out = cotangent[0].astype(jnp.float32)
    gate_dots = jnp.sum(grad_out[:, None, :] * per_choice, axis=2)
    grad_pick = gate_weights * (
        gate_dots - jnp.sum(gate_weights * gate_dots, axis=1, keepdims=True)
    )
    grad_logits = jnp.sum(grad_pick[:, :, None] * choose, axis=1)
    grad_choice = (
        (gate_weights[:, :, None] * grad_out[:, None, :])
        .astype(jnp.bfloat16)
        .reshape(2 * row_count, model_width)
    )
    padded_grads = jnp.concatenate([grad_choice, jnp.zeros((1, model_width), jnp.bfloat16)], axis=0)
    grad_slots = padded_grads[filler].reshape(MOST, expert_count, model_width)
    grad_arrived = lax.all_gather(grad_slots, ("ctx", "tp"), axis=0, tiled=True)
    grad_act = jnp.einsum(
        "sed,efd->sef", grad_arrived, down_again, preferred_element_type=jnp.float32
    )
    grad_down = jnp.einsum(
        "sef,sed->efd", activated, grad_arrived, preferred_element_type=jnp.float32
    )
    gelu_back = jax.vjp(jax.nn.gelu, pre_act)[1]
    grad_pre = gelu_back(grad_act)[0].astype(jnp.bfloat16)
    grad_up = jnp.einsum("sed,sef->edf", arrived, grad_pre, preferred_element_type=jnp.float32)
    row_block = grad_pre
    grad_dispatched = lax.psum_scatter(
        jnp.einsum("sef,edf->sed", row_block, up_again, preferred_element_type=jnp.float32),
        ("ctx", "tp"),
        scatter_dimension=0,
        tiled=True,
    )
    grad_normed_two = jnp.sum(
        grad_dispatched.reshape(MOST * expert_count, model_width)[position].reshape(
            row_count, 2, model_width
        ),
        axis=1,
    )
    router_float = router_again.astype(jnp.float32)
    grad_normed_two = grad_normed_two + jnp.dot(
        grad_logits, router_float.T, precision=lax.Precision.HIGHEST
    )
    grad_router = jnp.dot(
        normed_two.astype(jnp.float32).T, grad_logits, precision=lax.Precision.HIGHEST
    )
    weighted_two = grad_normed_two * gain_second.astype(jnp.float32)
    grad_gain_two = jnp.sum(grad_normed_two * middle * scale_two, axis=0)
    grad_middle = (
        grad_out
        + scale_two * weighted_two
        - middle * scale_two**3 * jnp.mean(weighted_two * middle, axis=1, keepdims=True)
    )
    grad_middle_low = grad_middle.astype(jnp.bfloat16)
    normed_group, grad_mid_group = (
        lax.all_gather(normed_one, "ctx", axis=0, tiled=True),
        lax.all_gather(grad_middle_low, "ctx", axis=0, tiled=True),
    )
    proj_rows = lax.dynamic_slice_in_dim(proj_again, ctx_index * head_width, head_width, 0)
    grad_attended = jnp.einsum(
        "te,de->td", grad_mid_group, proj_rows, preferred_element_type=jnp.float32
    ).astype(jnp.bfloat16)
    grad_proj_part = jnp.einsum(
        "td,te->de",
        attended_heads.reshape(length, head_width),
        grad_mid_group,
        preferred_element_type=jnp.float32,
    )
    grad_blocks = grad_attended.reshape(block_count, length, heads_here, head_size)

    def backward_block(running, pieces):
        key_sum, value_sum = running
        query_block, bias_block, mask_block, log_block, grad_block = pieces
        scores = block_scores(query_block, bias_block, mask_block)
        probs_float = jnp.exp(scores - log_block[..., None])
        low_probs = probs_float.astype(jnp.bfloat16)
        value_term = jnp.einsum(
            "hqk,qhd->khd", low_probs, grad_block, preferred_element_type=jnp.float32
        )
        grad_probs = jnp.einsum(
            "qhd,khd->hqk", grad_block, value_rows, preferred_element_type=jnp.float32
        )
        grad_scores = (
            probs_float * (grad_probs - jnp.sum(probs_float * grad_probs, axis=-1, keepdims=True))
        ).astype(jnp.bfloat16)
        query_term = (
            jnp.einsum("hqk,khd->qhd", grad_scores, key_rows, preferred_element_type=jnp.float32)
            * score_scale
        ).astype(jnp.bfloat16)
        key_term = (
            jnp.einsum("hqk,qhd->khd", grad_scores, query_block, preferred_element_type=jnp.float32)
            * score_scale
        )
        return ((key_sum + key_term, value_sum + value_term), (query_term, grad_scores))

    zero_rows = jnp.zeros((length, heads_here, head_size), jnp.float32)
    sums_kv, per_block = lax.scan(
        backward_block,
        (zero_rows, zero_rows),
        (query_blocks, bias_blocks, mask_blocks, log_totals, grad_blocks),
    )
    query_grads, score_grads = per_block
    grad_qkv_heads = jnp.stack(
        [
            query_grads.reshape(length, heads_here, head_size),
            sums_kv[0].astype(jnp.bfloat16),
            sums_kv[1].astype(jnp.bfloat16),
        ],
        axis=1,
    )
    grad_qkv_part = jnp.einsum(
        "td,tshk->dshk", normed_group, grad_qkv_heads, preferred_element_type=jnp.float32
    )
    grad_projected = lax.all_to_all(
        grad_qkv_heads, "ctx", split_axis=0, concat_axis=2, tiled=True
    ).reshape(row_count, 3 * model_width)
    score_matrix = (
        jnp.moveaxis(score_grads, 0, 1).reshape(heads_here, length, length).astype(jnp.float32)
    )
    spread_back = jax.vjp(spread_diagonals, bias_vector)[1]
    grad_vector = spread_back(score_matrix)[0]
    grad_table_here = jnp.dot(grad_vector, onehot, precision=lax.Precision.HIGHEST)
    table_term = lax.dynamic_update_slice_in_dim(
        jnp.zeros((head_count, BUCKETS), jnp.float32), grad_table_here, ctx_index * heads_here, 0
    )
    grad_normed_one = jnp.einsum(
        "te,de->td", grad_projected, qkv_again, preferred_element_type=jnp.float32
    )
    weighted_one = grad_normed_one * gain_first.astype(jnp.float32)
    grad_gain_one = jnp.sum(grad_normed_one * inputs * scale_one, axis=0)
    grad_tokens = (
        grad_middle
        + scale_one * weighted_one
        - inputs * scale_one**3 * jnp.mean(weighted_one * inputs, axis=1, keepdims=True)
    )
    shares = (
        lax.psum_scatter(grad_gain_one, "fsdp", scatter_dimension=0, tiled=True),
        lax.psum_scatter(grad_qkv_part, "fsdp", scatter_dimension=0, tiled=True),
        lax.psum_scatter(grad_proj_part, "fsdp", scatter_dimension=1, tiled=True),
        lax.psum_scatter(grad_router, "fsdp", scatter_dimension=0, tiled=True),
        lax.psum_scatter(grad_gain_two, "fsdp", scatter_dimension=0, tiled=True),
        lax.psum_scatter(grad_up, "fsdp", scatter_dimension=1, tiled=True),
        lax.psum_scatter(grad_down, "fsdp", scatter_dimension=2, tiled=True),
    )
    qkv_share = shares[1]
    own_rows = qkv_share.shape[0]
    qkv_placed = lax.dynamic_update_slice_in_dim(
        jnp.zeros((own_rows, 3, head_count, head_size), jnp.float32),
        qkv_share,
        ctx_index * heads_here,
        2,
    ).reshape(own_rows, 3 * model_width)
    proj_share = shares[2]
    proj_placed = lax.dynamic_update_slice_in_dim(
        jnp.zeros((model_width, proj_share.shape[1]), jnp.float32),
        proj_share,
        ctx_index * head_width,
        0,
    )
    summed = lax.psum((shares[0], qkv_placed, proj_placed, shares[3], shares[4]), ("ctx", "tp"))
    table_grad = lax.psum(table_term, ("fsdp", "ctx", "tp"))
    return (
        output,
        grad_tokens[None],
        summed[0],
        summed[1],
        summed[2],
        table_grad,
        summed[4],
        summed[3],
        shares[5],
        shares[6],
    )


def solution(mesh):
    in_specs = (
        P(("fsdp", "tp"), "ctx", None),
        P(("fsdp", "tp"), None),
        P(("fsdp", "tp"), "ctx", None),
        P("fsdp"),
        P("fsdp", None),
        P(None, "fsdp"),
        P(),
        P("fsdp"),
        P("fsdp", None),
        P(None, "fsdp", ("ctx", "tp")),
        P(None, ("ctx", "tp"), "fsdp"),
        P(("fsdp", "tp"), "ctx", None),
    )
    out_specs = (
        P(("fsdp", "tp"), "ctx", None),
        P(("fsdp", "tp"), "ctx", None),
        P("fsdp"),
        P("fsdp", None),
        P(None, "fsdp"),
        P(),
        P("fsdp"),
        P("fsdp", None),
        P(None, "fsdp", ("ctx", "tp")),
        P(None, ("ctx", "tp"), "fsdp"),
    )
    return jax.shard_map(local, mesh=mesh, in_specs=in_specs, out_specs=out_specs, check_vma=False)
```

profile of v0, /device:TPU:0, one launch (start us, length us, event | category | flops | bytes accessed | tf_op | source)
XLA Modules:
  0.0 897.2 jit_solution(6429418993881922095)
XLA Ops:
  11.4 5.2 all-gather
  16.7 4.4 all-gather.1
  27.6 7.1 copy.178
  34.7 6.6 slice.39
  41.3 13.2 %reshape.303 = f32[3,512,1023]{2,1,0:T(8,128)} reshape(f32[3,523776]{1,0:T(4,128)} %slice.39) | data formatting | bytes 12570624 | tf_op jit(solution)/shard_map/reshape | solution.py:40
  70.7 8.0 all-to-all-done
  88.4 4.0 all-to-all-start.1
  117.3 4.5 all_gather.44
  132.9 4.2 gather_fusion.2
  140.9 44.0 %all-gather.13.cloned.1.call-done = bf16[1280,4,768]{2,0,1:T(8,128)(2,1)} async-done(((bf16[80,4,768]{2,0,1:T(8,128)(2,1)}), bf16[1280,4,768]{2,0,1:T(8,128)(2,1)}) %all-gather.13.cloned.1.call-update) | async-done | bytes 7864336 | tf_op jit(solution)/shard_map/all_gather | solution.py:161
  184.9 8.1 fusion.63
  193.0 14.4 %all-gather.17.cloned.1.call-done = bf16[4,192,768]{2,1,0:T(8,128)(2,1)} async-done(((bf16[4,192,384]{2,1,0:T(8,128)(2,1)}), bf16[4,192,768]{2,1,0:T(8,128)(2,1)}) %all-gather.17.cloned.1.call-update) | async-done | bytes 1179664 | tf_op jit(solution)/shard_map/all_gather | solution.py:93
  207.5 10.3 %convolution_bitcast_fusion.1 = f32[1280,4,768]{2,0,1:T(8,128)} fusion(bf16[4,192,768]{2,1,0:T(8,128)(2,1)} %all-gather.17.cloned.1.call-done, f32[4,1280,192]{1,2,0:T(8,128)} %fusion.63), kind=kOutput, calls=%fused_computation.6 | convolution fusion | flops 1518796800 | bytes 20840448 | tf_op jit(solution)/shard_map/sef,efd->sed/dot_general | solution.py:166
  218.0 63.8 %all-gather.19.cloned.1.call-done = bf16[1280,4,768]{2,0,1:T(8,128)(2,1)} async-done(((bf16[80,4,768]{2,0,1:T(8,128)(2,1)}), bf16[1280,4,768]{2,0,1:T(8,128)(2,1)}) %all-gather.19.cloned.1.call-update) | async-done | bytes 7864336 | tf_op jit(solution)/shard_map/all_gather | solution.py:199
  281.9 8.6 fusion.6
  291.7 10.6 %convolution_bitcast_fusion = f32[1280,4,768]{2,0,1:T(8,128)} fusion(bf16[1280,4,192]{0,2,1:T(8,128)(2,1)S(1)} %fusion.6, bf16[4,768,192]{1,2,0:T(8,128)(2,1)S(1)} %copy-done.7), kind=kOutput, calls=%fused_computation.5 | convolution fusion | flops 1509949440 | bytes 18874368 | tf_op jit(solution)/shard_map/sef,edf->sed/dot_general | solution.py:211
  303.6 9.7 %all_gather.50 = bf16[512,768]{1,0:T(8,128)(2,1)} all-gather(bf16[128,768]{1,0:T(8,128)(2,1)} %copy-done.19), channel_id=1, replica_groups=mesh['fsdp'=2,'ctx'=4,'tp'=4] {'ctx'}, dimensions={0}, use_global_device_ids=true | all-gather | bytes 983040 | tf_op jit(solution)/shard_map/all_gather | solution.py:238
  314.0 127.2 %reduce-scatter.10.cloned.1.call-done = f32[80,4,768]{2,0,1:T(8,128)} async-done(((f32[1280,4,768]{2,0,1:T(8,128)}), f32[80,4,768]{2,0,1:T(8,128)}) %reduce-scatter.10.cloned.1.call-update) | async-done | bytes 983056 | tf_op jit(solution)/shard_map/reduce_scatter | solution.py:165
  459.1 142.7 %reduce-scatter.12.cloned.1.call-done = f32[80,4,768]{2,0,1:T(8,128)} async-done(((f32[1280,4,768]{2,0,1:T(8,128)}), f32[80,4,768]{2,0,1:T(8,128)}) %reduce-scatter.12.cloned.1.call-update) | async-done | bytes 983056 | tf_op jit(solution)/shard_map/reduce_scatter | solution.py:210
  620.4 8.6 all_gather.49
  648.1 28.3 %reduce-scatter.14.cloned.1.call-done = f32[384,3,3,64]{0,3,2,1:T(8,128)} async-done(((f32[768,3,3,64]{0,3,2,1:T(8,128)}), f32[384,3,3,64]{0,3,2,1:T(8,128)}) %reduce-scatter.14.cloned.1.call-update) | async-done | bytes 884752 | tf_op jit(solution)/shard_map/reduce_scatter | solution.py:320
  679.5 7.0 fusion.67
  688.0 7.8 fusion.57
  703.2 7.6 reshape.380
  710.9 5.7 reshape.314
  718.7 4.4 all-to-all-start.2
  723.1 4.6 pad_convert_fusion
  734.8 39.7 %psum.45 = f32[12,32]{1,0:T(8,128)} all-reduce(f32[12,32]{1,0:T(8,128)S(1)} %dynamic_update_slice.22), channel_id=1, replica_groups=mesh['fsdp'=2,'ctx'=4,'tp'=4] {'fsdp','ctx','tp'}, use_global_device_ids=true, to_apply=%region_30.31 | all-reduce | flops 384 | bytes 3072 | tf_op jit(solution)/shard_map/psum | solution.py:343
  786.7 5.3 all-reduce.9
  792.1 60.5 %all-reduce.7 = (f32[384]{0:T(512)}, f32[384]{0:T(512)}, f32[384,4]{0,1:T(4,128)}) all-reduce(f32[384]{0:T(512)S(1)} %dynamic-slice.3, f32[384]{0:T(512)S(1)} %dynamic-slice.5, f32[384,4]{0,1:T(4,128)S(1)} %copy.175), channel_id=1, replica_groups=mesh['fsdp'=2,'ctx'=4,'tp'=4] {'ctx','tp'}, use_global_device_ids=true, to_apply=%region_24.25 | all-reduce | flops 2304 | bytes 18432 | tf_op jit(solution)/shard_map/psum | solution.py:342
  855.4 5.2 copy.164
  860.6 28.8 %reduce-scatter.20.cloned.1.call-done = f32[4,192,384]{2,1,0:T(8,128)} async-done(((f32[4,192,768]{2,1,0:T(8,128)}), f32[4,192,384]{2,1,0:T(8,128)}) %reduce-scatter.20.cloned.1.call-update) | async-done | bytes 1179664 | tf_op jit(solution)/shard_map/reduce_scatter | solution.py:325
  (251 shorter events, 171.8 us)
Async XLA Ops:
  7.2 14.6 %copy-start = (f32[12,32]{1,0:T(8,128)S(1)}, f32[12,32]{1,0:T(8,128)}, u32[]{:S(2)}) copy-start(f32[12,32]{1,0:T(8,128)} %param.19) | copy-start | bytes 4612
  7.2 13.9 %copy-start.43 = (s32[31]{0:T(128)S(1)}, s32[31]{0:T(128)}, u32[]{:S(2)}) copy-start(s32[31]{0:T(128)} %constant.127.clone) | copy-start | bytes 376
  7.2 9.4 %copy-start.42 = (bf16[384]{0:T(512)(128)(2,1)S(1)}, bf16[384]{0:T(512)(128)(2,1)}, u32[]{:S(2)}) copy-start(bf16[384]{0:T(512)(128)(2,1)} %param.20) | copy-start | bytes 2308
  7.2 54.5 %all-gather.9.cloned.1.call-start = ((), (), s32[]{:S(2)}) async-start(), calls=%async_computation.10 | async-start | bytes 5308416 | tf_op jit(solution)/shard_map/all_gather | solution.py:88
  8.0 93.8 %all-gather.11.cloned.1.call-start = ((), (), s32[]{:S(2)}) async-start(), calls=%async_computation.11 | async-start | bytes 1769472 | tf_op jit(solution)/shard_map/all_gather | solution.py:89
  8.7 132.2 %all-gather.15.cloned.1.call-start = ((), (), s32[]{:S(2)}) async-start(), calls=%async_computation.13 | async-start | bytes 1769472 | tf_op jit(solution)/shard_map/all_gather | solution.py:92
  11.4 47.3 %copy-start.36 = (f32[128]{0:T(128)}, f32[128]{0:T(128)S(1)}, u32[]{:S(2)}) copy-start(f32[128]{0:T(128)S(1)} %get-tuple-element.139) | copy-start | bytes 1540
  16.7 42.1 %copy-start.26 = (f32[768]{0:T(1024)}, f32[768]{0:T(1024)S(1)}, u32[]{:S(2)}) copy-start(f32[768]{0:T(1024)S(1)} %reshape.367) | copy-start | bytes 9220
  60.7 9.1 %copy-start.33 = (s32[1,512]{1,0:T(1,128)S(1)}, s32[1,512]{1,0:T(1,128)}, u32[]{:S(2)}) copy-start(s32[1,512]{1,0:T(1,128)} %param.14) | copy-start | bytes 6148
  65.6 13.2 %all-to-all-start = ((bf16[128,3,12,64]{0,3,1,2:T(8,128)(2,1)}), bf16[128,3,12,64]{0,3,1,2:T(8,128)(2,1)S(1)}, u32[]{:S(2)}, u32[]{:S(2)}) async-start(bf16[128,3,12,64]{0,3,1,2:T(8,128)(2,1)} %copy.136), calls=%async_computation | async-start | bytes 1179648 | tf_op jit(solution)/shard_map/all_to_all | solution.py:102
  85.3 18.9 %copy-start.22 = (bf16[3,64,512]{2,1,0:T(8,128)(2,1)}, bf16[3,64,512]{2,1,0:T(8,128)(2,1)S(1)}, u32[]{:S(2)}) copy-start(bf16[3,64,512]{2,1,0:T(8,128)(2,1)S(1)} %fusion.19) | copy-start | bytes 589828
  88.4 9.4 %all-to-all-start.1 = ((bf16[4,2,12288]{2,1,0:T(2,128)(2,1)}), bf16[4,2,12288]{2,1,0:T(2,128)(2,1)}, u32[]{:S(2)}, u32[]{:S(2)}) async-start(bf16[4,2,12288]{2,1,0:T(2,128)(2,1)} %reshape.382), calls=%async_computation.1 | async-start | bytes 393216 | tf_op jit(solution)/shard_map/all_to_all | solution.py:144
  92.4 92.5 %all-gather.13.cloned.1.call-start = ((), (), s32[]{:S(2)}) async-start(), calls=%async_computation.12 | async-start | bytes 8355840 | tf_op jit(solution)/shard_map/all_gather | solution.py:161
  93.2 15.0 %copy-start.24 = (f32[768]{0:T(1024)}, f32[768]{0:T(1024)S(1)}, u32[]{:S(2)}) copy-start(f32[768]{0:T(1024)S(1)} %reshape.368) | copy-start | bytes 9220
  112.0 95.5 %all-gather.17.cloned.1.call-start = ((), (), s32[]{:S(2)}) async-start(), calls=%async_computation.14 | async-start | bytes 1769472 | tf_op jit(solution)/shard_map/all_gather | solution.py:93
  112.6 169.3 %all-gather.19.cloned.1.call-start = ((), (), s32[]{:S(2)}) async-start(), calls=%async_computation.16 | async-start | bytes 8355840 | tf_op jit(solution)/shard_map/all_gather | solution.py:199
  121.7 15.3 %copy-start.28 = (bf16[768,4]{0,1:T(4,128)(2,1)}, bf16[768,4]{0,1:T(4,128)(2,1)S(1)}, u32[]{:S(2)}) copy-start(bf16[768,4]{0,1:T(4,128)(2,1)S(1)} %all_gather.44) | copy-start | bytes 18436
  140.9 300.3 %reduce-scatter.10.cloned.1.call-start = ((), (), s32[]{:S(2)}) async-start(), calls=%async_computation.15 | async-start | bytes 16711680 | tf_op jit(solution)/shard_map/reduce_scatter | solution.py:165
  217.8 384.0 %reduce-scatter.12.cloned.1.call-start = ((), (), s32[]{:S(2)}) async-start(), calls=%async_computation.17 | async-start | bytes 16711680 | tf_op jit(solution)/shard_map/reduce_scatter | solution.py:210
  281.9 9.8 %copy-start.7 = (bf16[4,768,192]{1,2,0:T(8,128)(2,1)S(1)}, bf16[4,768,192]{1,2,0:T(8,128)(2,1)}, u32[]{:S(2)}) copy-start(bf16[4,768,192]{1,2,0:T(8,128)(2,1)} %all-gather.15.cloned.1.call-done) | copy-start | bytes 3538948
  302.3 343.0 %reduce-scatter.16.cloned.1.call-start = ((), (), s32[]{:S(2)}) async-start(), calls=%async_computation.19 | async-start | bytes 884736 | tf_op jit(solution)/shard_map/reduce_scatter | solution.py:321
  616.0 13.8 %copy-start.23 = (bf16[3,64,512]{2,1,0:T(8,128)(2,1)S(1)}, bf16[3,64,512]{2,1,0:T(8,128)(2,1)}, u32[]{:S(2)}) copy-start(bf16[3,64,512]{2,1,0:T(8,128)(2,1)} %copy-done.22) | copy-start | bytes 589828
  631.0 45.4 %reduce-scatter.14.cloned.1.call-start = ((), (), s32[]{:S(2)}) async-start(), calls=%async_computation.18 | async-start | bytes 2654208 | tf_op jit(solution)/shard_map/reduce_scatter | solution.py:320
  640.2 134.3 %reduce-scatter.22.cloned.1.call-start = ((), (), s32[]{:S(2)}) async-start(), calls=%async_computation.22 | async-start | bytes 589824
  641.4 214.0 %all-reduce.12.cloned.1.call-start = ((), (), s32[]{:S(2)}) async-start(), calls=%async_computation.23 | async-start | bytes 9437184 | tf_op jit(solution)/shard_map/psum | solution.py:342
  679.5 181.2 %reduce-scatter.18.cloned.1.call-start = ((), (), s32[]{:S(2)}) async-start(), calls=%async_computation.20 | async-start | bytes 3538944 | tf_op jit(solution)/shard_map/reduce_scatter | solution.py:324
  686.5 202.9 %reduce-scatter.20.cloned.1.call-start = ((), (), s32[]{:S(2)}) async-start(), calls=%async_computation.21 | async-start | bytes 3538944 | tf_op jit(solution)/shard_map/reduce_scatter | solution.py:325
  718.7 56.8 %all-to-all-start.2 = ((bf16[4,2,36864]{2,1,0:T(2,128)(2,1)}), bf16[4,2,36864]{2,1,0:T(2,128)(2,1)}, u32[]{:S(2)}, u32[]{:S(2)}) async-start(bf16[4,2,36864]{2,1,0:T(2,128)(2,1)} %reshape.384), calls=%async_computation.4 | async-start | bytes 1179648 | tf_op jit(solution)/shard_map/all_to_all | solution.py:296
  731.0 51.8 %copy-start.4 = (bf16[768,2304]{1,0:T(8,128)(2,1)S(1)}, bf16[768,2304]{1,0:T(8,128)(2,1)}, u32[]{:S(2)}) copy-start(bf16[768,2304]{1,0:T(8,128)(2,1)} %all-gather.9.cloned.1.call-done) | copy-start | bytes 10616836
  731.0 51.8 %copy-start.27 = (f32[768]{0:T(1024)S(1)}, f32[768]{0:T(1024)}, u32[]{:S(2)}) copy-start(f32[768]{0:T(1024)} %copy-done.26) | copy-start | bytes 9220
  855.4 35.1 %copy-start.1 = (f32[12,32]{1,0:T(8,128)S(1)}, f32[12,32]{1,0:T(8,128)}, u32[]{:S(2)}) copy-start(f32[12,32]{1,0:T(8,128)} %param.19) | copy-start | bytes 4612
  855.4 34.1 %copy-start.20 = (f32[768,384]{1,0:T(8,128)S(1)}, f32[768,384]{1,0:T(8,128)}, u32[]{:S(2)}) copy-start(f32[768,384]{1,0:T(8,128)} %get-tuple-element.156) | copy-start | bytes 3538948
  (31 other events, 93.1 us)
Sparse Core Ops, SparseCore 0:
  9.6 52.0 all-gather.8
  63.3 22.7 all-gather.10
  87.7 22.7 all-gather.14
  113.3 71.5 all-gather.12
  186.3 21.1 all-gather.16
  210.2 71.5 all-gather.18
  286.0 155.1 reduce-scatter.9
  445.8 155.9 reduce-scatter.11
  631.1 14.1 reduce-scatter.15
  648.1 28.2 reduce-scatter.13
  678.6 13.0 reduce-scatter.21
  696.3 118.0 all-reduce.11
  817.3 34.6 reduce-scatter.17
  854.7 34.7 reduce-scatter.19
where the time goes:
time: 905 us; the launch traced here: 897 us
  waiting for transfers between devices  468 us (52%)
  local copies, waits for them, and re-layouts  146 us (16%)
  blocking collectives  138 us (15%)
  matrix products  79.4 us (9%)
  other arithmetic  37 us (4%)
  between operations  15.4 us (2%)
  starting transfers between devices  13.4 us (1%)
    reduce_scatter x1, waiting for transfers between devices, local(): lax.psum_scatter(jnp.einsum('sef,edf->sed', row_block, up_again, preferre...  143 us
    reduce_scatter x1, waiting for transfers between devices, local(): lax.psum_scatter(jnp.einsum('sef,efd->sed', row_block, down_full, preferr...  127 us
    all_gather x1, waiting for transfers between devices, local(): grad_arrived = lax.all_gather(grad_slots, ('ctx', 'tp'), axis=0, tiled=True)  63.8 us
    psum x1, blocking collectives, local(): lax.psum((shares[0], qkv_placed, proj_placed, shares[3], shares[4]), ('ct...  60.5 us
    unnamed x108, local copies, waits for them, and re-layouts  51.7 us
    all_gather x1, waiting for transfers between devices, local(): arrived = lax.all_gather(dispatched, ('ctx', 'tp'), axis=0, tiled=True)  44 us
    psum x1, blocking collectives, local(): table_grad = lax.psum(table_term, ('fsdp', 'ctx', 'tp'))  39.7 us
    reduce_scatter x1, waiting for transfers between devices, local(): lax.psum_scatter(grad_down, 'fsdp', scatter_dimension=2, tiled=True)  28.8 us
  transfers between devices with their start and end apart: 17, of which 11 were waited for; matrix products, arithmetic and copies ran while one was open for 25% of the time, Pallas kernels for 0%

commit v1 on v0

--- a/solution.py
+++ b/solution.py
@@ -340,7 +340,8 @@
         0,
     )
     summed = lax.psum((shares[0], qkv_placed, proj_placed, shares[3], shares[4]), ("ctx", "tp"))
-    table_grad = lax.psum(table_term, ("fsdp", "ctx", "tp"))
+    parts = lax.all_gather(table_term, ("fsdp", "ctx", "tp"))
+    table_grad = jnp.sum(parts, axis=0)
     return (
         output,
         grad_tokens[None],

time: 905 us -> 912 us (level)
  blocking collectives: 138 us -> 172 us
  waiting for transfers between devices: 468 us -> 440 us
    all_gather x0 -> x1, blocking collectives: none -> 76.4 us  [local(): parts = lax.all_gather(table_term, ('fsdp', 'ctx', 'tp'))]
    psum x1 -> x0, blocking collectives: 39.7 us -> none  [local(): table_grad = lax.psum(table_term, ('fsdp', 'ctx', 'tp'))]
    reduce_scatter x1, waiting for transfers between devices: 28.8 us -> 0.01 us  [local(): lax.psum_scatter(grad_down, 'fsdp', scatter_dimension=2, tiled=True)]
  transfers between devices with their start and end apart: 17 -> 17, of which waited for: 11 -> 10; matrix products, arithmetic and copies ran while one was open for 25% -> 25% of each run, Pallas kernels for 0% -> 0%
where the time goes in v1:
time: 912 us; the launch traced here: 904 us
  waiting for transfers between devices  440 us (48%)
  blocking collectives  172 us (19%)
  local copies, waits for them, and re-layouts  146 us (16%)
  matrix products  79.3 us (9%)
  other arithmetic  38.6 us (4%)
  between operations  15.4 us (2%)
  starting transfers between devices  13.7 us (2%)
    reduce_scatter x1, waiting for transfers between devices, local(): lax.psum_scatter(jnp.einsum('sef,edf->sed', row_block, up_again, preferre...  143 us
    reduce_scatter x1, waiting for transfers between devices, local(): lax.psum_scatter(jnp.einsum('sef,efd->sed', row_block, down_full, preferr...  127 us
    all_gather x1, blocking collectives, local(): parts = lax.all_gather(table_term, ('fsdp', 'ctx', 'tp'))  76.4 us
    all_gather x1, waiting for transfers between devices, local(): grad_arrived = lax.all_gather(grad_slots, ('ctx', 'tp'), axis=0, tiled=True)  63.9 us
    psum x1, blocking collectives, local(): lax.psum((shares[0], qkv_placed, proj_placed, shares[3], shares[4]), ('ct...  58 us
    unnamed x108, local copies, waits for them, and re-layouts  51.7 us
    all_gather x1, waiting for transfers between devices, local(): arrived = lax.all_gather(dispatched, ('ctx', 'tp'), axis=0, tiled=True)  43.6 us
    reduce_scatter x1, waiting for transfers between devices, local(): lax.psum_scatter(grad_qkv_part, 'fsdp', scatter_dimension=0, tiled=True)  28.4 us
  transfers between devices with their start and end apart: 17, of which 10 were waited for; matrix products, arithmetic and copies ran while one was open for 25% of the time, Pallas kernels for 0%

profile of v1, /device:TPU:0, one launch (start us, length us, event | category | flops | bytes accessed | tf_op | source)
XLA Modules:
  0.0 904.1 jit_solution(570262049001624554)
XLA Ops:
  11.4 5.2 all-gather
  16.7 4.4 all-gather.1
  27.6 7.1 copy.178
  34.7 6.4 slice.39
  41.1 13.2 %reshape.305 = f32[3,512,1023]{2,1,0:T(8,128)} reshape(f32[3,523776]{1,0:T(4,128)} %slice.39) | data formatting | bytes 12570624 | tf_op jit(solution)/shard_map/reshape | solution.py:40
  65.6 4.0 all-to-all-start
  71.1 8.0 all-to-all-done
  117.6 4.5 all_gather.50
  133.2 4.2 gather_fusion.2
  141.3 43.6 %all-gather.13.cloned.1.call-done = bf16[1280,4,768]{2,0,1:T(8,128)(2,1)} async-done(((bf16[80,4,768]{2,0,1:T(8,128)(2,1)}), bf16[1280,4,768]{2,0,1:T(8,128)(2,1)}) %all-gather.13.cloned.1.call-update) | async-done | bytes 7864336 | tf_op jit(solution)/shard_map/all_gather | solution.py:161
  184.9 8.1 fusion.62
  193.0 14.4 %all-gather.17.cloned.1.call-done = bf16[4,192,768]{2,1,0:T(8,128)(2,1)} async-done(((bf16[4,192,384]{2,1,0:T(8,128)(2,1)}), bf16[4,192,768]{2,1,0:T(8,128)(2,1)}) %all-gather.17.cloned.1.call-update) | async-done | bytes 1179664 | tf_op jit(solution)/shard_map/all_gather | solution.py:93
  207.5 10.3 %convolution_bitcast_fusion.1 = f32[1280,4,768]{2,0,1:T(8,128)} fusion(bf16[4,192,768]{2,1,0:T(8,128)(2,1)} %all-gather.17.cloned.1.call-done, f32[4,1280,192]{1,2,0:T(8,128)} %fusion.62), kind=kOutput, calls=%fused_computation.6 | convolution fusion | flops 1518796800 | bytes 20840448 | tf_op jit(solution)/shard_map/sef,efd->sed/dot_general | solution.py:166
  218.0 63.9 %all-gather.19.cloned.1.call-done = bf16[1280,4,768]{2,0,1:T(8,128)(2,1)} async-done(((bf16[80,4,768]{2,0,1:T(8,128)(2,1)}), bf16[1280,4,768]{2,0,1:T(8,128)(2,1)}) %all-gather.19.cloned.1.call-update) | async-done | bytes 7864336 | tf_op jit(solution)/shard_map/all_gather | solution.py:199
  281.9 8.6 fusion.6
  291.7 10.6 %convolution_bitcast_fusion = f32[1280,4,768]{2,0,1:T(8,128)} fusion(bf16[1280,4,192]{0,2,1:T(8,128)(2,1)S(1)} %fusion.6, bf16[4,768,192]{1,2,0:T(8,128)(2,1)S(1)} %copy-done.7), kind=kOutput, calls=%fused_computation.5 | convolution fusion | flops 1509949440 | bytes 18874368 | tf_op jit(solution)/shard_map/sef,edf->sed/dot_general | solution.py:211
  303.6 9.7 %all_gather.56 = bf16[512,768]{1,0:T(8,128)(2,1)} all-gather(bf16[128,768]{1,0:T(8,128)(2,1)} %copy-done.19), channel_id=1, replica_groups=mesh['fsdp'=2,'ctx'=4,'tp'=4] {'ctx'}, dimensions={0}, use_global_device_ids=true | all-gather | bytes 983040 | tf_op jit(solution)/shard_map/all_gather | solution.py:238
  314.0 127.2 %reduce-scatter.10.cloned.1.call-done = f32[80,4,768]{2,0,1:T(8,128)} async-done(((f32[1280,4,768]{2,0,1:T(8,128)}), f32[80,4,768]{2,0,1:T(8,128)}) %reduce-scatter.10.cloned.1.call-update) | async-done | bytes 983056 | tf_op jit(solution)/shard_map/reduce_scatter | solution.py:165
  459.1 142.7 %reduce-scatter.12.cloned.1.call-done = f32[80,4,768]{2,0,1:T(8,128)} async-done(((f32[1280,4,768]{2,0,1:T(8,128)}), f32[80,4,768]{2,0,1:T(8,128)}) %reduce-scatter.12.cloned.1.call-update) | async-done | bytes 983056 | tf_op jit(solution)/shard_map/reduce_scatter | solution.py:210
  620.4 8.6 all_gather.55
  641.2 4.1 reduce-scatter.16.cloned.1.call-done
  648.1 28.4 %reduce-scatter.14.cloned.1.call-done = f32[384,3,3,64]{0,3,2,1:T(8,128)} async-done(((f32[768,3,3,64]{0,3,2,1:T(8,128)}), f32[384,3,3,64]{0,3,2,1:T(8,128)}) %reduce-scatter.14.cloned.1.call-update) | async-done | bytes 884752 | tf_op jit(solution)/shard_map/reduce_scatter | solution.py:320
  679.6 7.0 fusion.66
  688.3 7.8 fusion.56
  703.4 7.6 reshape.382
  711.0 5.7 reshape.316
  718.9 4.3 all-to-all-start.2
  723.2 4.6 pad_convert_fusion
  734.9 76.4 %all_gather.58 = f32[32,12,32]{2,1,0:T(8,128)} all-gather(f32[1,12,32]{2,1,0:T(8,128)S(1)} %dynamic_update_slice.23), channel_id=1, replica_groups=mesh['fsdp'=2,'ctx'=4,'tp'=4] {'fsdp','ctx','tp'}, dimensions={0}, use_global_device_ids=true | all-gather | bytes 50688 | tf_op jit(solution)/shard_map/all_gather | solution.py:343
  825.0 5.2 all-reduce.9
  830.4 58.0 %all-reduce.7 = (f32[384]{0:T(512)}, f32[384]{0:T(512)}, f32[384,4]{0,1:T(4,128)}) all-reduce(f32[384]{0:T(512)S(1)} %dynamic-slice.3, f32[384]{0:T(512)S(1)} %dynamic-slice.5, f32[384,4]{0,1:T(4,128)S(1)} %copy.175), channel_id=1, replica_groups=mesh['fsdp'=2,'ctx'=4,'tp'=4] {'ctx','tp'}, use_global_device_ids=true, to_apply=%region_24.25 | all-reduce | flops 2304 | bytes 18432 | tf_op jit(solution)/shard_map/psum | solution.py:342
  891.1 5.2 copy.164
  (252 shorter events, 169.7 us)
Async XLA Ops:
  7.2 14.6 %copy-start = (f32[12,32]{1,0:T(8,128)S(1)}, f32[12,32]{1,0:T(8,128)}, u32[]{:S(2)}) copy-start(f32[12,32]{1,0:T(8,128)} %param.19) | copy-start | bytes 4612
  7.2 13.9 %copy-start.43 = (s32[31]{0:T(128)S(1)}, s32[31]{0:T(128)}, u32[]{:S(2)}) copy-start(s32[31]{0:T(128)} %constant.128.clone) | copy-start | bytes 376
  7.2 9.4 %copy-start.42 = (bf16[384]{0:T(512)(128)(2,1)S(1)}, bf16[384]{0:T(512)(128)(2,1)}, u32[]{:S(2)}) copy-start(bf16[384]{0:T(512)(128)(2,1)} %param.20) | copy-start | bytes 2308
  7.2 54.5 %all-gather.9.cloned.1.call-start = ((), (), s32[]{:S(2)}) async-start(), calls=%async_computation.10 | async-start | bytes 5308416 | tf_op jit(solution)/shard_map/all_gather | solution.py:88
  8.0 94.2 %all-gather.11.cloned.1.call-start = ((), (), s32[]{:S(2)}) async-start(), calls=%async_computation.11 | async-start | bytes 1769472 | tf_op jit(solution)/shard_map/all_gather | solution.py:89
  8.7 132.6 %all-gather.15.cloned.1.call-start = ((), (), s32[]{:S(2)}) async-start(), calls=%async_computation.13 | async-start | bytes 1769472 | tf_op jit(solution)/shard_map/all_gather | solution.py:92
  11.4 47.2 %copy-start.36 = (f32[128]{0:T(128)}, f32[128]{0:T(128)S(1)}, u32[]{:S(2)}) copy-start(f32[128]{0:T(128)S(1)} %get-tuple-element.139) | copy-start | bytes 1540
  16.7 41.9 %copy-start.26 = (f32[768]{0:T(1024)}, f32[768]{0:T(1024)S(1)}, u32[]{:S(2)}) copy-start(f32[768]{0:T(1024)S(1)} %reshape.369) | copy-start | bytes 9220
  60.5 9.7 %copy-start.33 = (s32[1,512]{1,0:T(1,128)S(1)}, s32[1,512]{1,0:T(1,128)}, u32[]{:S(2)}) copy-start(s32[1,512]{1,0:T(1,128)} %param.14) | copy-start | bytes 6148
  65.6 13.5 %all-to-all-start = ((bf16[128,3,12,64]{0,3,1,2:T(8,128)(2,1)}), bf16[128,3,12,64]{0,3,1,2:T(8,128)(2,1)S(1)}, u32[]{:S(2)}, u32[]{:S(2)}) async-start(bf16[128,3,12,64]{0,3,1,2:T(8,128)(2,1)} %copy.136), calls=%async_computation | async-start | bytes 1179648 | tf_op jit(solution)/shard_map/all_to_all | solution.py:102
  85.6 18.9 %copy-start.22 = (bf16[3,64,512]{2,1,0:T(8,128)(2,1)}, bf16[3,64,512]{2,1,0:T(8,128)(2,1)S(1)}, u32[]{:S(2)}) copy-start(bf16[3,64,512]{2,1,0:T(8,128)(2,1)S(1)} %fusion.19) | copy-start | bytes 589828
  88.8 9.4 %all-to-all-start.1 = ((bf16[4,2,12288]{2,1,0:T(2,128)(2,1)}), bf16[4,2,12288]{2,1,0:T(2,128)(2,1)}, u32[]{:S(2)}, u32[]{:S(2)}) async-start(bf16[4,2,12288]{2,1,0:T(2,128)(2,1)} %reshape.384), calls=%async_computation.1 | async-start | bytes 393216 | tf_op jit(solution)/shard_map/all_to_all | solution.py:144
  92.8 92.1 %all-gather.13.cloned.1.call-start = ((), (), s32[]{:S(2)}) async-start(), calls=%async_computation.12 | async-start | bytes 8355840 | tf_op jit(solution)/shard_map/all_gather | solution.py:161
  93.5 15.0 %copy-start.24 = (f32[768]{0:T(1024)}, f32[768]{0:T(1024)S(1)}, u32[]{:S(2)}) copy-start(f32[768]{0:T(1024)S(1)} %reshape.370) | copy-start | bytes 9220
  112.3 95.1 %all-gather.17.cloned.1.call-start = ((), (), s32[]{:S(2)}) async-start(), calls=%async_computation.14 | async-start | bytes 1769472 | tf_op jit(solution)/shard_map/all_gather | solution.py:93
  112.9 168.9 %all-gather.19.cloned.1.call-start = ((), (), s32[]{:S(2)}) async-start(), calls=%async_computation.16 | async-start | bytes 8355840 | tf_op jit(solution)/shard_map/all_gather | solution.py:199
  122.1 15.3 %copy-start.28 = (bf16[768,4]{0,1:T(4,128)(2,1)}, bf16[768,4]{0,1:T(4,128)(2,1)S(1)}, u32[]{:S(2)}) copy-start(bf16[768,4]{0,1:T(4,128)(2,1)S(1)} %all_gather.50) | copy-start | bytes 18436
  141.2 300.0 %reduce-scatter.10.cloned.1.call-start = ((), (), s32[]{:S(2)}) async-start(), calls=%async_computation.15 | async-start | bytes 16711680 | tf_op jit(solution)/shard_map/reduce_scatter | solution.py:165
  217.8 384.0 %reduce-scatter.12.cloned.1.call-start = ((), (), s32[]{:S(2)}) async-start(), calls=%async_computation.17 | async-start | bytes 16711680 | tf_op jit(solution)/shard_map/reduce_scatter | solution.py:210
  281.9 9.8 %copy-start.7 = (bf16[4,768,192]{1,2,0:T(8,128)(2,1)S(1)}, bf16[4,768,192]{1,2,0:T(8,128)(2,1)}, u32[]{:S(2)}) copy-start(bf16[4,768,192]{1,2,0:T(8,128)(2,1)} %all-gather.15.cloned.1.call-done) | copy-start | bytes 3538948
  302.3 343.0 %reduce-scatter.16.cloned.1.call-start = ((), (), s32[]{:S(2)}) async-start(), calls=%async_computation.19 | async-start | bytes 884736 | tf_op jit(solution)/shard_map/reduce_scatter | solution.py:321
  607.1 8.9 copy-start.11
  607.1 8.9 copy-start.25
  616.0 13.8 %copy-start.23 = (bf16[3,64,512]{2,1,0:T(8,128)(2,1)S(1)}, bf16[3,64,512]{2,1,0:T(8,128)(2,1)}, u32[]{:S(2)}) copy-start(bf16[3,64,512]{2,1,0:T(8,128)(2,1)} %copy-done.22) | copy-start | bytes 589828
  631.0 45.5 %reduce-scatter.14.cloned.1.call-start = ((), (), s32[]{:S(2)}) async-start(), calls=%async_computation.18 | async-start | bytes 2654208 | tf_op jit(solution)/shard_map/reduce_scatter | solution.py:320
  640.0 173.0 %reduce-scatter.22.cloned.1.call-start = ((), (), s32[]{:S(2)}) async-start(), calls=%async_computation.22 | async-start | bytes 589824
  641.2 249.9 %all-reduce.12.cloned.1.call-start = ((), (), s32[]{:S(2)}) async-start(), calls=%async_computation.23 | async-start | bytes 9437184 | tf_op jit(solution)/shard_map/psum | solution.py:342
  679.5 216.8 %reduce-scatter.18.cloned.1.call-start = ((), (), s32[]{:S(2)}) async-start(), calls=%async_computation.20 | async-start | bytes 3538944 | tf_op jit(solution)/shard_map/reduce_scatter | solution.py:324
  686.6 209.7 %reduce-scatter.20.cloned.1.call-start = ((), (), s32[]{:S(2)}) async-start(), calls=%async_computation.21 | async-start | bytes 3538944 | tf_op jit(solution)/shard_map/reduce_scatter | solution.py:325
  718.9 95.1 %all-to-all-start.2 = ((bf16[4,2,36864]{2,1,0:T(2,128)(2,1)}), bf16[4,2,36864]{2,1,0:T(2,128)(2,1)}, u32[]{:S(2)}, u32[]{:S(2)}) async-start(bf16[4,2,36864]{2,1,0:T(2,128)(2,1)} %reshape.386), calls=%async_computation.4 | async-start | bytes 1179648 | tf_op jit(solution)/shard_map/all_to_all | solution.py:296
  731.1 90.1 %copy-start.4 = (bf16[768,2304]{1,0:T(8,128)(2,1)S(1)}, bf16[768,2304]{1,0:T(8,128)(2,1)}, u32[]{:S(2)}) copy-start(bf16[768,2304]{1,0:T(8,128)(2,1)} %all-gather.9.cloned.1.call-done) | copy-start | bytes 10616836
  731.1 90.1 %copy-start.27 = (f32[768]{0:T(1024)S(1)}, f32[768]{0:T(1024)}, u32[]{:S(2)}) copy-start(f32[768]{0:T(1024)} %copy-done.26) | copy-start | bytes 9220
  (31 other events, 87.0 us)
Sparse Core Ops, SparseCore 0:
  9.6 52.0 all-gather.8
  63.3 22.7 all-gather.10
  87.7 22.7 all-gather.14
  113.3 71.5 all-gather.12
  186.3 21.1 all-gather.16
  210.2 71.5 all-gather.18
  286.0 155.1 reduce-scatter.9
  445.8 155.9 reduce-scatter.11
  631.1 14.1 reduce-scatter.15
  648.1 28.3 reduce-scatter.13
  678.7 13.0 reduce-scatter.21
  696.4 119.0 all-reduce.11
  818.4 34.4 reduce-scatter.17
  855.6 34.6 reduce-scatter.19
